TPU v7x, 256 devices: a whole 4x4x8 slice. The times are simulated.
256 devices in a mesh: dp: 32 (over z, x_hi, core), tensor: 8 (over y, x_lo).
Axes of the slice: x: 4 (x_hi: 2, x_lo: 2; x = x_hi * 2 + x_lo), y: 4, z: 8, core: 2. Of those that a mesh axis runs over, the one named last changes fastest.
Arguments:
- context: bfloat16 [12288, 8192], P('dp', 'tensor'), may hold values from -6 to 6
- output_weight: bfloat16 [8192, 8192], P('tensor', 'dp'), may hold values from -0.0625 to 0.0625
- adapter_down_weight: bfloat16 [8192, 16], P('tensor'), may hold values from -0.0625 to 0.0625
- adapter_up_weight: bfloat16 [16, 8192], replicated, may hold values from -0.29882812 to 0.29882812
- residual: bfloat16 [12288, 8192], P('dp', 'tensor'), may hold values from -60 to 60
- frozen_residual_delta: bfloat16 [12288, 8192], P('dp', 'tensor'), may hold values from -6 to 6
- harmful_count: int32 [32], replicated, may hold values from 48 to 192
- retain_count: int32 [32], replicated, may hold values from 48 to 192
Outputs:
- adapted: bfloat16 [12288, 8192], P('dp', 'tensor')
- grad_a: float32 [8192, 16], P('tensor')
- grad_b: float32 [16, 8192], replicated
All inputs are finite; a program needn't handle non-finite values.
Results may differ from a plain program's by a relative error of at most 0.005.
Values may be sent and summed in bfloat16 or wider, within the bound.
A program may use at most 128 MiB of HBM per device.

v0:
```python
import jax
import jax.numpy as jnp
from jax import lax
from jax.sharding import PartitionSpec as P

ADAPTER_SCALE = 2.0
NORM_EPS = 1e-06
REROUTE_WEIGHT = 65536.0
RETAIN_WEIGHT = 1024.0


def row_gradient(
    hidden_states,
    target,
    sq_state,
    sq_target,
    cross_term,
    gap_sq,
    harmful,
    retained,
    harm_total,
    keep_total,
):
    norm_h = jnp.sqrt(sq_state + NORM_EPS)
    norm_g = jnp.sqrt(sq_target + NORM_EPS)
    cosine = cross_term / (norm_h * norm_g)
    distance = jnp.sqrt(gap_sq + NORM_EPS)
    weight_harm = REROUTE_WEIGHT / harm_total * harmful
    weight_keep = RETAIN_WEIGHT / keep_total * retained
    first = (weight_harm / (norm_h * norm_g))[:, None] * target
    second = (weight_harm * cosine / (norm_h * norm_h))[:, None] * hidden_states
    third = (weight_keep / distance)[:, None] * (hidden_states - target)
    return first - second + third


def token_masks(positions, harm_here, keep_here):
    harmful = (positions < harm_here).astype(jnp.float32)
    retained = ((positions >= harm_here) & (positions < harm_here + keep_here)).astype(jnp.float32)
    return (harmful, retained)


def head_terms(context, output_weight):
    return jnp.dot(
        context,
        lax.all_gather(output_weight, "dp", axis=1, tiled=True),
        preferred_element_type=jnp.float32,
    )


def local(
    context,
    output_weight,
    adapter_down_weight,
    adapter_up_weight,
    residual,
    frozen_residual_delta,
    harmful_count,
    retain_count,
):
    seq_len = context.shape[0]
    tensor_rank = lax.axis_index("tensor")
    data_rank = lax.axis_index("dp")
    harm_total = jnp.sum(harmful_count).astype(jnp.float32)
    keep_total = jnp.sum(retain_count).astype(jnp.float32)
    harm_here = harmful_count[data_rank]
    keep_here = retain_count[data_rank]
    up_weight_single = adapter_up_weight.astype(jnp.float32)
    reduced_state = lax.psum(
        jnp.dot(context, adapter_down_weight, preferred_element_type=jnp.float32), "tensor"
    )
    attn_cols = lax.psum_scatter(
        head_terms(context, output_weight).astype(jnp.bfloat16),
        "tensor",
        scatter_dimension=1,
        tiled=True,
    ).astype(jnp.float32)
    col_count = attn_cols.shape[1]
    up_weight_columns = lax.dynamic_slice_in_dim(
        up_weight_single, tensor_rank * col_count, col_count, 1
    )
    hidden_states = (
        residual.astype(jnp.float32)
        + attn_cols
        + ADAPTER_SCALE * jnp.dot(reduced_state, up_weight_columns, precision=lax.Precision.HIGHEST)
    )
    target = residual.astype(jnp.float32) + frozen_residual_delta.astype(jnp.float32)
    gap = hidden_states - target
    sq_state, sq_target, cross_term, gap_sq = lax.psum(
        (
            jnp.sum(hidden_states * hidden_states, axis=1),
            jnp.sum(target * target, axis=1),
            jnp.sum(hidden_states * target, axis=1),
            jnp.sum(gap * gap, axis=1),
        ),
        "tensor",
    )
    positions = jnp.arange(seq_len, dtype=jnp.int32)
    harmful, retained = token_masks(positions, harm_here, keep_here)
    output_gradient = row_gradient(
        hidden_states,
        target,
        sq_state,
        sq_target,
        cross_term,
        gap_sq,
        harmful,
        retained,
        harm_total,
        keep_total,
    )
    reduced_gradient = lax.psum(
        ADAPTER_SCALE
        * jnp.dot(output_gradient, up_weight_columns.T, precision=lax.Precision.HIGHEST),
        "tensor",
    )
    local_a = jnp.dot(
        context.T,
        reduced_gradient,
        precision=lax.Precision.HIGHEST,
        preferred_element_type=jnp.float32,
    )
    shard_up_weight = ADAPTER_SCALE * jnp.dot(
        reduced_state.T, output_gradient, precision=lax.Precision.HIGHEST
    )
    grad_a, grad_b_cols = lax.psum((local_a, shard_up_weight), "dp")
    grad_b = lax.all_gather(grad_b_cols, "tensor", axis=1, tiled=True)
    adapted = hidden_states.astype(jnp.bfloat16)
    return (adapted, grad_a, grad_b)


def solution(mesh):
    return jax.shard_map(
        local,
        mesh=mesh,
        in_specs=(
            P("dp", "tensor"),
            P("tensor", "dp"),
            P("tensor", None),
            P(),
            P("dp", "tensor"),
            P("dp", "tensor"),
            P(),
            P(),
        ),
        out_specs=(P("dp", "tensor"), P("tensor", None), P()),
        check_vma=False,
    )
```

profile of v0, /device:TPU:1, one launch (start us, length us, event | category | flops | bytes accessed | tf_op | source)
XLA Modules:
  0.0 653.9 jit_solution(2326122769122141415)
XLA Ops:
  7.2 0.0 copy-start
  7.2 0.0 all-gather.2.cloned.1.call-start
  7.2 0.7 all-gather.2.cloned.1.call-update
  7.9 0.0 reduce-scatter.2.cloned.1.call-start
  8.0 158.7 %all-gather.2.cloned.1.call-done = bf16[1024,8192]{1,0:T(8,128)(2,1)} async-done(((bf16[1024,256]{1,0:T(8,128)(2,1)}), bf16[1024,8192]{1,0:T(8,128)(2,1)}) %all-gather.2.cloned.1.call-update) | async-done | bytes 16777232 | tf_op jit(solution)/shard_map/all_gather | solution.py:45
  166.7 0.0 copy-done
  166.7 14.4 %convolution_convert_fusion = bf16[384,8192]{1,0:T(8,128)(2,1)} fusion(bf16[384,1024]{1,0:T(8,128)(2,1)S(1)} %copy-done, bf16[1024,8192]{1,0:T(8,128)(2,1)} %all-gather.2.cloned.1.call-done), kind=kOutput, calls=%fused_computation | convolution fusion | flops 6445596672 | bytes 23855104 | tf_op jit(solution)/shard_map/dot_general | solution.py:43
  181.0 0.0 copy-start.3
  181.0 0.0 copy-start.4
  181.0 0.0 copy-start.2
  181.0 0.0 copy-start.1
  181.0 0.0 reduce-scatter.2.cloned.1.call-update
  181.1 0.0 all-reduce.4.cloned.1.call-start
  181.1 0.6 copy-done.3
  181.7 0.6 reduce_sum.58
  182.3 0.6 dynamic_slice.11
  183.0 0.0 copy-done.4
  183.0 0.6 reduce_sum.54
  183.6 0.6 dynamic_slice.10
  186.8 0.0 copy-done.2
  186.9 0.3 fusion.8
  187.2 29.8 %psum.56 = f32[384,16]{0,1:T(8,128)S(1)} all-reduce(f32[384,16]{0,1:T(8,128)S(1)} %fusion.8), channel_id=1, replica_groups=mesh['dp'=32,'tensor'=8] {'tensor'}, use_global_device_ids=true, to_apply=%region_1.0 | all-reduce | flops 6144 | bytes 49152 | tf_op jit(solution)/shard_map/psum | solution.py:68
  217.0 93.3 %reduce-scatter.2.cloned.1.call-done = bf16[384,1024]{1,0:T(8,128)(2,1)} async-done(((bf16[384,8192]{1,0:T(8,128)(2,1)}), bf16[384,1024]{1,0:T(8,128)(2,1)}) %reduce-scatter.2.cloned.1.call-update) | async-done | bytes 786448 | tf_op jit(solution)/shard_map/reduce_scatter | solution.py:71
  310.3 0.0 copy-done.1
  310.3 3.1 multiply_reduce_fusion.1
  313.4 14.6 %all-reduce.1 = (f32[384]{0:T(512)S(1)}, f32[384]{0:T(512)S(1)}, f32[384]{0:T(512)S(1)}, f32[384]{0:T(512)S(1)}) all-reduce(f32[384]{0:T(512)S(1)} %get-tuple-element.4, f32[384]{0:T(512)S(1)} %get-tuple-element.3, f32[384]{0:T(512)S(1)} %get-tuple-element.6, f32[384]{0:T(512)S(1)} %get-tuple-element.5), channel_id=1, replica_groups=mesh['dp'=32,'tensor'=8] {'tensor'}, use_global_device_ids=true, to_apply=%region_11.0 | all-reduce | flops 1536 | bytes 12288 | tf_op jit(solution)/shard_map/psum | solution.py:88
  328.0 0.7 select_divide_fusion
  328.7 2.7 multiply_add_fusion
  331.4 1.5 convolution_multiply_fusion.1
  332.9 1.6 convolution_multiply_fusion
  334.5 27.2 %psum.61 = f32[384,16]{1,0:T(8,128)S(1)} all-reduce(f32[384,16]{1,0:T(8,128)S(1)} %convolution_multiply_fusion), channel_id=1, replica_groups=mesh['dp'=32,'tensor'=8] {'tensor'}, use_global_device_ids=true, to_apply=%region_12.0 | all-reduce | flops 6144 | bytes 49152 | tf_op jit(solution)/shard_map/psum | solution.py:111
  361.7 1.1 convolution_bitcast_fusion
  362.8 0.0 all-reduce.4.cloned.1.call-update
  362.8 258.1 %all-reduce.4.cloned.1.call-done = (f32[1024,16]{0,1:T(8,128)}, f32[16,1024]{1,0:T(8,128)}) async-done(((f32[1024,16]{0,1:T(8,128)}, f32[16,1024]{1,0:T(8,128)}), (f32[1024,16]{0,1:T(8,128)}, f32[16,1024]{1,0:T(8,128)})) %all-reduce.4.cloned.1.call-update) | async-done | bytes 131088 | tf_op jit(solution)/shard_map/psum | solution.py:125
  620.9 24.2 %all_gather.7 = f32[16,8192]{1,0:T(8,128)S(1)} all-gather(f32[16,1024]{1,0:T(8,128)} %get-tuple-element.8), channel_id=1, replica_groups=mesh['dp'=32,'tensor'=8] {'tensor'}, dimensions={1}, use_global_device_ids=true | all-gather | bytes 589824 | tf_op jit(solution)/shard_map/all_gather | solution.py:126
  645.1 1.5 copy.14
  646.6 0.8 copy.15
Async XLA Ops:
  7.2 159.5 %copy-start = (bf16[384,1024]{1,0:T(8,128)(2,1)S(1)}, bf16[384,1024]{1,0:T(8,128)(2,1)}, u32[]{:S(2)}) copy-start(bf16[384,1024]{1,0:T(8,128)(2,1)} %param.8) | copy-start | bytes 2359300
  7.2 159.5 %all-gather.2.cloned.1.call-start = ((), (), s32[]{:S(2)}) async-start(), calls=%async_computation.1 | async-start | bytes 17301504 | tf_op jit(solution)/shard_map/all_gather | solution.py:45
  7.9 302.3 %reduce-scatter.2.cloned.1.call-start = ((), (), s32[]{:S(2)}) async-start(), calls=%async_computation.2 | async-start | bytes 7077888 | tf_op jit(solution)/shard_map/reduce_scatter | solution.py:71
  181.0 0.7 copy-start.3
  181.0 1.9 copy-start.4
  181.0 5.8 copy-start.2
  181.0 129.2 %copy-start.1 = (bf16[384,1024]{1,0:T(8,128)(2,1)S(1)}, bf16[384,1024]{1,0:T(8,128)(2,1)}, u32[]{:S(2)}) copy-start(bf16[384,1024]{1,0:T(8,128)(2,1)} %param.13) | copy-start | bytes 2359300
  181.1 439.9 %all-reduce.4.cloned.1.call-start = ((), (), s32[]{:S(2)}) async-start(), calls=%async_computation.3 | async-start | bytes 262144 | tf_op jit(solution)/shard_map/psum | solution.py:125
Sparse Core Ops, SparseCore 0:
  10.5 156.0 all-gather.1
  181.2 129.0 reduce-scatter.1
  362.9 257.9 all-reduce.3
where the time goes:
time: 660 us; the launch traced here: 654 us
  waiting for transfers between devices  511 us (77%)
  blocking collectives  95.8 us (15%)
  matrix products  22 us (3%)
  between operations  16.5 us (2%)
    psum x1, waiting for transfers between devices, local(): grad_a, grad_b_cols = lax.psum((local_a, shard_up_weight), 'dp')  258 us
    all_gather x1, waiting for transfers between devices, head_terms(): lax.all_gather(output_weight, 'dp', axis=1, tiled=True)  159 us
    reduce_scatter x1, waiting for transfers between devices, local(): lax.psum_scatter(head_terms(context, output_weight).astype(jnp.bfloat16),...  93.3 us
    psum x1, blocking collectives, local(): lax.psum(jnp.dot(context, adapter_down_weight, preferred_element_type=jnp...  29.8 us
    psum x1, blocking collectives, local(): lax.psum(ADAPTER_SCALE * jnp.dot(output_gradient, up_weight_columns.T, pr...  27.2 us
    all_gather x1, blocking collectives, local(): grad_b = lax.all_gather(grad_b_cols, 'tensor', axis=1, tiled=True)  24.2 us
    psum x1, blocking collectives, local(): lax.psum((jnp.sum(hidden_states * hidden_states, axis=1), jnp.sum(target...  14.6 us
    dot_general x1, matrix products, head_terms(): jnp.dot(context, lax.all_gather(output_weight, 'dp', axis=1, tiled=True),...  14.4 us
  transfers between devices with their start and end apart: 3, of which 3 were waited for; matrix products, arithmetic and copies ran while one was open for 0% of the time, Pallas kernels for 0%

commit v1 on v0

v1 whole, which is shorter than its diff:
```python
import jax
import jax.numpy as jnp
from jax import lax
from jax.experimental import pallas as pl
from jax.experimental.pallas import tpu as pltpu
from jax.sharding import PartitionSpec as P

NORM_EPS = 1e-06
REROUTE_WEIGHT = 65536.0
RETAIN_WEIGHT = 1024.0

NZ = 8
NY = 4
NX = 4
NT = 8
NDP = 32
LEN = 384
HALF = LEN // 2
KB = 1024
RANK = 16
F32 = jnp.float32
BF16 = jnp.bfloat16
NT_DIMS = (((1,), (1,)), ((), ()))
TN_DIMS = (((0,), (0,)), ((), ()))
NN_DIMS = (((1,), (0,)), ((), ()))


def split3(value):
    hi = value.astype(BF16)
    rest = value - hi.astype(F32)
    mid = rest.astype(BF16)
    low = (rest - mid.astype(F32)).astype(BF16)
    return jnp.concatenate([hi, mid, low], axis=0)


def fold3(value):
    return value[0:RANK] + value[RANK : 2 * RANK] + value[2 * RANK : 3 * RANK]


def dot32(a, b, dims):
    return lax.dot_general(a, b, dims, preferred_element_type=F32)


def dot_high(a, b, dims):
    return lax.dot_general(a, b, dims, precision=lax.Precision.HIGHEST, preferred_element_type=F32)


def kernel(
    ctx_hbm,
    w_hbm,
    down_ref,
    up_hbm,
    res_hbm,
    dlt_hbm,
    harm_ref,
    keep_ref,
    adapted_hbm,
    ga_ref,
    gb_ref,
    a_buf,
    w_buf,
    p_buf,
    r_buf,
    xs_buf,
    xr_buf,
    up_buf,
    res_buf,
    dlt_buf,
    ad_buf,
    ghi_buf,
    glo_buf,
    early_send,
    early_recv,
    late_send,
    late_recv,
    g_send,
    g_recv,
    h_send,
    h_recv,
    b_recv,
    acc_buf,
    in_sem,
    out_sem,
    a_send,
    a_sem,
    w_send,
    w_sem,
    p_send,
    r_sem,
    x_send,
    x_sem,
    small_send,
    early_sem,
    late_sem,
    g_sem,
    h_sem,
    b_sem,
):
    dp = lax.axis_index("dp")
    t = lax.axis_index("tensor")
    z = dp // 4
    xh = (dp // 2) % 2
    c = dp % 2
    y = t // 2
    xl = t % 2
    x = 2 * xh + xl
    right = (x + 1) % NX
    left = (x + 3) % NX

    def dev(z_to, y_to, x_to, c_to):
        return (z_to * 4 + (x_to // 2) * 2 + c_to, y_to * 2 + x_to % 2)

    def remote(src, dst, send, recv, to):
        return pltpu.make_async_remote_copy(
            src_ref=src,
            dst_ref=dst,
            send_sem=send,
            recv_sem=recv,
            device_id=to,
            device_id_type=pl.DeviceIdType.MESH,
        )

    def wait_copy(ref, sem):
        pltpu.make_async_copy(ref, ref, sem).wait()

    def wait_all(ref, sems, count):
        @pl.loop(0, count)
        def _(source):
            wait_copy(ref.at[source], sems.at[source])

    to_right = dev(z, y, right, c)
    to_left = dev(z, y, left, c)
    to_core = dev(z, y, x, 1 - c)
    to_pair = dev(z, y, 2 * xh + (1 - xl), c)
    to_up = dev((z + 1) % NZ, y, x, c)
    to_down = dev((z + 7) % NZ, y, x, c)

    def a_index(x_of, c_of):
        return (x_of % 2) * 4 + (x_of // 2) * 2 + c_of

    own = a_index(x, c)
    own_a = pltpu.make_async_copy(ctx_hbm, a_buf.at[own], in_sem.at[0])
    own_a.start()
    own_w = pltpu.make_async_copy(
        w_hbm.at[:, pl.ds(pl.multiple_of(xl * 128, 128), 128)], w_buf.at[xl], w_sem.at[0]
    )
    own_w.start()
    load_up = pltpu.make_async_copy(
        up_hbm.at[:, pl.ds(pl.multiple_of(t * KB, KB), KB)], up_buf, in_sem.at[1]
    )
    load_up.start()
    load_res = pltpu.make_async_copy(res_hbm, res_buf, in_sem.at[2])
    load_res.start()
    load_dlt = pltpu.make_async_copy(dlt_hbm, dlt_buf, in_sem.at[3])
    load_dlt.start()

    barrier = pltpu.get_barrier_semaphore()

    def greet(to):
        pl.semaphore_signal(barrier, inc=1, device_id=to, device_id_type=pl.DeviceIdType.MESH)

    for step in range(1, NY):
        greet(dev(z, (y + step) % NY, x, 1 - c))
    greet(dev(z, y, 2 * (1 - xh) + (1 - xl), c))
    for step in range(1, NT):
        greet((dp, (t + step) % NT))

    @pl.loop(1, NDP)
    def _(step):
        greet(((dp + step) % NDP, t))

    pl.semaphore_wait(barrier, (NY - 1) + 1 + (NT - 1) + (NDP - 1))

    send_pair = remote(
        w_hbm.at[:, pl.ds(pl.multiple_of((1 - xl) * 128, 128), 128)],
        w_buf.at[xl],
        w_send,
        w_sem.at[1],
        to_pair,
    )
    send_pair.start()

    def send_a_rows(block, rows, sem, to):
        return remote(
            a_buf.at[block, pl.ds(rows * HALF, HALF)],
            a_buf.at[block, pl.ds(rows * HALF, HALF)],
            a_send,
            a_sem.at[sem],
            to,
        )

    def send_a_block(block, sem, to):
        return remote(a_buf.at[block], a_buf.at[block], a_send, a_sem.at[sem], to)

    def wait_a_rows(block, rows, sem):
        ref = a_buf.at[block, pl.ds(rows * HALF, HALF)]
        pltpu.make_async_copy(ref, ref, a_sem.at[sem]).wait()

    def wait_a_block(block, sem):
        ref = a_buf.at[block]
        pltpu.make_async_copy(ref, ref, a_sem.at[sem]).wait()

    own_a.wait()
    send_a_rows(own, 0, 1, to_right).start()
    send_a_rows(own, 1, 4, to_left).start()
    send_a_rows(own, 1, 2, to_right).start()
    send_a_rows(own, 0, 3, to_left).start()
    send_a_block(own, 0, to_core).start()

    def wait_w(slot, part):
        ref = w_buf.at[slot * 2 + (xl + part) % 2]
        pltpu.make_async_copy(ref, ref, w_sem.at[slot * 2 + part]).wait()

    def send_w(slot, part, to_slot, to):
        row = (xl + part) % 2
        remote(
            w_buf.at[slot * 2 + row],
            w_buf.at[to_slot * 2 + row],
            w_send,
            w_sem.at[to_slot * 2 + part],
            to,
        ).start()

    wait_w(0, 0)
    send_w(0, 0, 1, to_up)
    send_w(0, 0, 2, to_down)

    load_up.wait()
    load_res.wait()
    load_dlt.wait()
    early_send[0:RANK] = dot32(down_ref[...], a_buf[own], NT_DIMS)
    early_send[RANK : 2 * RANK] = dot32(up_buf[...], res_buf[...], NT_DIMS) + dot32(
        up_buf[...], dlt_buf[...], NT_DIMS
    )
    ones = jnp.ones((8, 128), F32)
    acc_buf[0] = jnp.zeros((LEN, 128), F32)
    for j in range(8):
        cols = pl.ds(j * 128, 128)
        target = res_buf[:, cols].astype(F32) + dlt_buf[:, cols].astype(F32)
        acc_buf[0] += target * target
    early_send[2 * RANK :] = dot_high(ones, acc_buf[0], NT_DIMS)
    for step in range(1, NT):
        remote(
            early_send, early_recv.at[t], small_send.at[0], early_sem.at[t], (dp, (t + step) % NT)
        ).start()
    pltpu.make_async_copy(early_send, early_recv.at[t], early_sem.at[t]).start()

    wait_w(0, 1)
    send_w(0, 1, 1, to_up)
    send_w(0, 1, 2, to_down)

    def forward(slot, part, to_slot, to):
        wait_w(slot, part)
        send_w(slot, part, to_slot, to)

    def multiply(xh_of, slots):
        total = None
        for k in range(2):
            rows = a_buf[pl.ds(k * 4 + xh_of * 2, 2)].reshape(2 * LEN, KB)
            cols = [w_buf[slot * 2 + k] for slot in slots]
            cols = cols[0] if len(cols) == 1 else jnp.concatenate(cols, axis=1)
            part = dot32(rows, cols, NN_DIMS)
            total = part if total is None else total + part
        for i, slot in enumerate(slots):
            p_buf[pl.ds(slot * 4 + xh_of * 2, 2)] = (
                total[:, i * 128 : (i + 1) * 128].astype(BF16).reshape(2, LEN, 128)
            )
        offset = {0: 0, 1: 7, 2: 1, 3: 6, 4: 2, 5: 5, 6: 3, 7: 4}
        for slot in slots:
            owner = (z + offset[slot]) % NZ
            y_to = owner // 2
            group = (owner % 2) * 2 + xh_of
            for c_of in range(2):
                src = p_buf.at[slot * 4 + xh_of * 2 + c_of]
                dst = r_buf.at[group, y * 2 + c]
                here = (y_to == y) & (c_of == c)

                @pl.when(here)
                def _():
                    pltpu.make_async_copy(src, dst, r_sem.at[group, y * 2 + c]).start()

                @pl.when(jnp.logical_not(here))
                def _():
                    remote(
                        src, dst, p_send, r_sem.at[group, y * 2 + c], dev(z, y_to, x, c_of)
                    ).start()

    forward(1, 0, 3, to_up)
    forward(2, 0, 4, to_down)
    wait_a_rows(a_index(left, c), 0, 1)
    send_a_rows(a_index(left, c), 0, 5, to_right).start()
    wait_a_rows(a_index(right, c), 1, 4)
    send_a_rows(a_index(right, c), 1, 6, to_left).start()
    forward(1, 1, 3, to_up)
    forward(2, 1, 4, to_down)
    wait_a_rows(a_index(left, c), 1, 2)
    send_a_block(a_index(left, c), 7, to_core).start()
    wait_a_rows(a_index(right, c), 0, 3)
    send_a_block(a_index(right, c), 8, to_core).start()
    forward(3, 0, 5, to_up)
    forward(4, 0, 6, to_down)
    wait_a_block(a_index(x, 1 - c), 0)
    wait_a_block(a_index(left, 1 - c), 7)
    wait_a_block(a_index(right, 1 - c), 8)
    multiply(xh, (0,))
    multiply(xh, (1, 2))
    forward(3, 1, 5, to_up)
    forward(4, 1, 6, to_down)
    multiply(xh, (3, 4))
    wait_a_rows(a_index((x + 2) % NX, c), 0, 5)
    wait_a_rows(a_index((x + 2) % NX, c), 1, 6)
    send_a_block(a_index((x + 2) % NX, c), 9, to_core).start()
    forward(5, 0, 7, to_up)
    wait_w(6, 0)
    wait_a_block(a_index((x + 2) % NX, 1 - c), 9)
    multiply(1 - xh, (0,))
    multiply(1 - xh, (1, 2))
    multiply(1 - xh, (3, 4))
    wait_w(5, 1)
    forward(6, 1, 7, to_down)
    multiply(1 - xh, (5, 6))
    multiply(xh, (5, 6))
    wait_w(7, 0)
    wait_w(7, 1)
    multiply(1 - xh, (7,))
    multiply(xh, (7,))

    for xh_of in range(2):
        for xl_of in range(2):
            group = xl_of * 2 + xh_of
            x_to = xh_of * 2 + xl_of
            for source in range(8):
                wait_copy(r_buf.at[group, source], r_sem.at[group, source])
            for c_of in range(2):
                total = r_buf[group, c_of].astype(F32)
                for y_of in range(1, NY):
                    total = total + r_buf[group, y_of * 2 + c_of].astype(F32)
                xs_buf[x_to, c_of] = total.astype(BF16)

            @pl.when(x_to == x)
            def _():
                pltpu.make_async_copy(xs_buf.at[x_to], xr_buf.at[x], x_sem.at[x]).start()

            @pl.when(x_to != x)
            def _():
                remote(
                    xs_buf.at[x_to], xr_buf.at[x], x_send, x_sem.at[x], dev(z, y, x_to, c)
                ).start()

    wait_all(early_recv, early_sem, NT)
    early = early_recv[0]
    for other in range(1, NT):
        early = early + early_recv[other]
    low_rank = early[0:RANK]
    target_up = early[RANK : 2 * RANK]
    sq_target = early[2 * RANK : 2 * RANK + 1]
    low3 = split3(2.0 * low_rank)

    for source in range(NX):
        wait_copy(xr_buf.at[source], x_sem.at[source])
    for i in range(3):
        acc_buf[i] = jnp.zeros((LEN, 128), F32)
    for j in range(8):
        cols = pl.ds(j * 128, 128)
        x_of = (j // 4) * 2 + j % 2
        c_of = (j // 2) % 2
        up3 = jnp.concatenate([up_buf[:, cols]] * 3, axis=0)
        res = res_buf[:, cols].astype(F32)
        state = res + xr_buf[x_of, c_of].astype(F32) + dot32(low3, up3, TN_DIMS)
        ad_buf[:, cols] = state.astype(BF16)
        target = res + dlt_buf[:, cols].astype(F32)
        gap = state - target
        acc_buf[0] += state * state
        acc_buf[1] += state * target
        acc_buf[2] += gap * gap
        high = gap.astype(BF16)
        ghi_buf[:, cols] = high
        glo_buf[:, cols] = (gap - high.astype(F32)).astype(BF16)
    store_adapted = pltpu.make_async_copy(ad_buf, adapted_hbm, out_sem)
    store_adapted.start()
    late_send[0:RANK] = dot32(up_buf[...], ghi_buf[...], NT_DIMS) + dot32(
        up_buf[...], glo_buf[...], NT_DIMS
    )
    for i in range(3):
        late_send[RANK + 8 * i : RANK + 8 * i + 8] = dot_high(ones, acc_buf[i], NT_DIMS)
    for step in range(1, NT):
        remote(
            late_send, late_recv.at[t], small_send.at[1], late_sem.at[t], (dp, (t + step) % NT)
        ).start()
    pltpu.make_async_copy(late_send, late_recv.at[t], late_sem.at[t]).start()

    rank = lax.broadcasted_iota(jnp.int32, (1, NDP), 1)

    def total_and_here(count_ref):
        count = count_ref[...].astype(F32)
        here = jnp.where(rank == dp, count, 0.0)
        return jnp.sum(count, axis=1, keepdims=True), jnp.sum(here, axis=1, keepdims=True)

    harm_sum, harm_here = total_and_here(harm_ref)
    keep_sum, keep_here = total_and_here(keep_ref)
    position = lax.broadcasted_iota(jnp.int32, (1, LEN), 1).astype(F32)
    harmful = (position < harm_here).astype(F32)
    retained = ((position >= harm_here) & (position < harm_here + keep_here)).astype(F32)
    weight_harm = REROUTE_WEIGHT / harm_sum * harmful
    weight_keep = RETAIN_WEIGHT / keep_sum * retained

    wait_all(late_recv, late_sem, NT)
    late = late_recv[0]
    for other in range(1, NT):
        late = late + late_recv[other]
    gap_up = late[0:RANK]
    norm_h = jnp.sqrt(late[RANK : RANK + 1] + NORM_EPS)
    cross = late[RANK + 8 : RANK + 9]
    distance = jnp.sqrt(late[RANK + 16 : RANK + 17] + NORM_EPS)
    norm_g = jnp.sqrt(sq_target + NORM_EPS)
    cosine = cross / (norm_h * norm_g)
    first = weight_harm / (norm_h * norm_g)
    second = weight_harm * cosine / (norm_h * norm_h)
    third = weight_keep / distance
    by_target = 2.0 * (first - second)
    by_gap = 2.0 * (third - second)
    low_cot = by_target * target_up + by_gap * gap_up
    ga = fold3(dot32(split3(low_cot), a_buf[own], NN_DIMS))
    left_side = split3(low_rank * by_target)
    right_side = split3(low_rank * by_gap)
    gb = fold3(
        dot32(left_side, res_buf[...], NN_DIMS)
        + dot32(left_side, dlt_buf[...], NN_DIMS)
        + dot32(right_side, ghi_buf[...], NN_DIMS)
        + dot32(right_side, glo_buf[...], NN_DIMS)
    )
    for j in range(8):
        g_send[0:RANK, j, :] = ga[:, j * 128 : (j + 1) * 128]
        g_send[RANK:, j, :] = gb[:, j * 128 : (j + 1) * 128]

    @pl.loop(1, NDP)
    def _(step):
        to = (dp + step) % NDP
        remote(g_send.at[to], g_recv.at[dp], small_send.at[2], g_sem.at[dp], (to, t)).start()

    pltpu.make_async_copy(g_send.at[dp], g_recv.at[dp], g_sem.at[dp]).start()
    wait_all(g_recv, g_sem, NDP)
    total = g_recv[0]
    for other in range(1, NDP):
        total = total + g_recv[other]
    h_send[...] = total

    @pl.loop(1, NDP)
    def _(step):
        remote(
            h_send, h_recv.at[dp], small_send.at[3], h_sem.at[dp], ((dp + step) % NDP, t)
        ).start()

    pltpu.make_async_copy(h_send, h_recv.at[dp], h_sem.at[dp]).start()
    wait_all(h_recv, h_sem, NDP)
    gb_rows = h_recv.at[pl.ds(RANK, RANK)]
    for step in range(1, NT):
        remote(gb_rows, b_recv.at[t], small_send.at[4], b_sem.at[t], (dp, (t + step) % NT)).start()
    pltpu.make_async_copy(gb_rows, b_recv.at[t], b_sem.at[t]).start()
    for j in range(8):
        ga_ref[:, j * 128 : (j + 1) * 128] = h_recv[0:RANK, j, :]
    wait_all(b_recv, b_sem, NT)
    for t_of in range(NT):
        for j in range(8):
            start = t_of * KB + j * 128
            gb_ref[:, start : start + 128] = b_recv[t_of, :, j, :]

    wait_copy(a_buf.at[pl.ds(0, 7)], a_send)
    wait_copy(w_buf.at[pl.ds(0, 15)], w_send)
    wait_copy(p_buf.at[pl.ds(0, 28)], p_send)
    wait_copy(xs_buf.at[pl.ds(0, 3)], x_send)
    wait_copy(early_recv.at[pl.ds(0, NT - 1)], small_send.at[0])
    wait_copy(late_recv.at[pl.ds(0, NT - 1)], small_send.at[1])
    wait_copy(g_recv.at[pl.ds(0, NDP - 1)], small_send.at[2])
    wait_copy(h_recv.at[pl.ds(0, NDP - 1)], small_send.at[3])
    wait_copy(b_recv.at[pl.ds(0, NT - 1)], small_send.at[4])
    store_adapted.wait()


def local(ctx, w, down, up, res, dlt, harm, keep):
    vmem = pl.BlockSpec(memory_space=pltpu.VMEM)
    anyw = pl.BlockSpec(memory_space=pl.ANY)
    adapted, ga, gb = pl.pallas_call(
        kernel,
        out_shape=(
            jax.ShapeDtypeStruct((LEN, KB), BF16),
            jax.ShapeDtypeStruct((RANK, KB), F32),
            jax.ShapeDtypeStruct((RANK, NT * KB), F32),
        ),
        in_specs=[anyw, anyw, vmem, anyw, anyw, anyw, vmem, vmem],
        out_specs=(anyw, vmem, vmem),
        scratch_shapes=[
            pltpu.VMEM((8, LEN, KB), BF16),
            pltpu.VMEM((16, KB, 128), BF16),
            pltpu.VMEM((32, LEN, 128), BF16),
            pltpu.VMEM((4, 8, LEN, 128), BF16),
            pltpu.VMEM((4, 2, LEN, 128), BF16),
            pltpu.VMEM((4, 2, LEN, 128), BF16),
            pltpu.VMEM((RANK, KB), BF16),
            pltpu.VMEM((LEN, KB), BF16),
            pltpu.VMEM((LEN, KB), BF16),
            pltpu.VMEM((LEN, KB), BF16),
            pltpu.VMEM((LEN, KB), BF16),
            pltpu.VMEM((LEN, KB), BF16),
            pltpu.VMEM((40, LEN), F32),
            pltpu.VMEM((NT, 40, LEN), F32),
            pltpu.VMEM((40, LEN), F32),
            pltpu.VMEM((NT, 40, LEN), F32),
            pltpu.VMEM((NDP, 8, 128), F32),
            pltpu.VMEM((NDP, 8, 128), F32),
            pltpu.VMEM((8, 128), F32),
            pltpu.VMEM((NDP, 8, 128), F32),
            pltpu.VMEM((NT, RANK, 8, 128), F32),
            pltpu.VMEM((3, LEN, 128), F32),
            pltpu.SemaphoreType.DMA((4,)),
            pltpu.SemaphoreType.DMA,
            pltpu.SemaphoreType.DMA,
            pltpu.SemaphoreType.DMA((10,)),
            pltpu.SemaphoreType.DMA,
            pltpu.SemaphoreType.DMA((16,)),
            pltpu.SemaphoreType.DMA,
            pltpu.SemaphoreType.DMA((4, 8)),
            pltpu.SemaphoreType.DMA,
            pltpu.SemaphoreType.DMA((NX,)),
            pltpu.SemaphoreType.DMA((5,)),
            pltpu.SemaphoreType.DMA((NT,)),
            pltpu.SemaphoreType.DMA((NT,)),
            pltpu.SemaphoreType.DMA((NDP,)),
            pltpu.SemaphoreType.DMA((NDP,)),
            pltpu.SemaphoreType.DMA((NT,)),
        ],
        compiler_params=pltpu.CompilerParams(
            collective_id=0, has_side_effects=True, vmem_limit_bytes=56 * 1024 * 1024
        ),
    )(ctx, w, down.T, up, res, dlt, harm.reshape(1, NDP), keep.reshape(1, NDP))
    return adapted, ga.T, gb


def solution(mesh):
    return jax.shard_map(
        local,
        mesh=mesh,
        in_specs=(
            P("dp", "tensor"),
            P("tensor", "dp"),
            P("tensor", None),
            P(),
            P("dp", "tensor"),
            P("dp", "tensor"),
            P(),
            P(),
        ),
        out_specs=(P("dp", "tensor"), P("tensor", None), P()),
        check_vma=False,
    )
```

time: 660 us -> 148 us (0.22)
  waiting for transfers between devices: 511 us -> 0 us
  Pallas kernels: 0 us -> 143 us
  blocking collectives: 95.8 us -> 0 us
  matrix products: 22 us -> 0 us
  between operations: 16.5 us -> 0.66 us
    psum x1 -> x0, waiting for transfers between devices: 258 us -> none  [local(): grad_a, grad_b_cols = lax.psum((local_a, shard_up_weight), 'dp')]
    all_gather x1 -> x0, waiting for transfers between devices: 159 us -> none  [head_terms(): lax.all_gather(output_weight, 'dp', axis=1, tiled=True)]
    pallas_call x0 -> x1, Pallas kernels: none -> 143 us  [local(): pl.pallas_call(kernel, out_shape=(jax.ShapeDtypeStruct((LEN, KB), BF16),...]
    reduce_scatter x1 -> x0, waiting for transfers between devices: 93.3 us -> none  [local(): lax.psum_scatter(head_terms(context, output_weight).astype(jnp.bfloat16),...]
    psum x3 -> x0, blocking collectives: 71.6 us -> none  [the longest x1 29.8 us: local(): lax.psum(jnp.dot(context, adapter_down_weight, preferred_element_type=jnp...]
    all_gather x1 -> x0, blocking collectives: 24.2 us -> none  [local(): grad_b = lax.all_gather(grad_b_cols, 'tensor', axis=1, tiled=True)]
    dot_general x6 -> x0, matrix products: 22 us -> none  [the longest x1 14.4 us: head_terms(): jnp.dot(context, lax.all_gather(output_weight, 'dp', axis=1, tiled=True),...]
  transfers between devices with their start and end apart: 3 -> 0, of which waited for: 3 -> 0; matrix products, arithmetic and copies ran while one was open for 0% -> 0% of each run, Pallas kernels for 0% -> 0%
where the time goes in v1:
time: 148 us
  Pallas kernels  143 us (97%)
  local copies, waits for them, and re-layouts  3.55 us (2%)
    pallas_call x1, Pallas kernels, local(): pl.pallas_call(kernel, out_shape=(jax.ShapeDtypeStruct((LEN, KB), BF16),...  143 us
    unnamed x7, local copies, waits for them, and re-layouts  3.55 us

profile of v1, /device:TPU:1, one launch (start us, length us, event | category | flops | bytes accessed | tf_op | source)
XLA Modules:
  0.0 147.6 jit_solution(7540643056930105430)
XLA Ops:
  0.6 143.3 %shard_map.103 = (bf16[384,1024]{1,0:T(8,128)(2,1)}, f32[16,1024]{1,0:T(8,128)}, f32[16,8192]{1,0:T(8,128)}) custom-call(bf16[384,1024]{1,0:T(8,128)(2,1)} %ctx_hbm.1, bf16[1024,256]{1,0:T(8,128)(2,1)} %w_hbm.1, bf16[16,1024]{1,0:T(8,128)(2,1)} %bitcast.5, bf16[16,8192]{1,0:T(8,128)(2,1)} %up_hbm.1, bf16[384,1024]{1,0:T(8,128)(2,1)} %res_hbm.1, ...), custom_call_target="tpu_custom_call" | custom-call | tf_op jit(solution)/shard_map/pallas_call | solution.py:483
  144.0 0.0 copy-start.1
  144.0 0.0 copy-start
  144.0 2.1 %copy.14 = bf16[384,1024]{1,0:T(8,128)(2,1)} copy(bf16[384,1024]{1,0:T(8,128)(2,1)} %get-tuple-element.12) | data formatting | bytes 1572864
  146.1 0.0 copy-done.1
  146.1 0.6 copy.15
  146.8 0.0 copy-done
  146.8 0.8 copy.16
Async XLA Ops:
  144.0 2.1 %copy-start.1 = (f32[16,1024]{1,0:T(8,128)S(1)}, f32[16,1024]{1,0:T(8,128)}, u32[]{:S(2)}) copy-start(f32[16,1024]{1,0:T(8,128)} %get-tuple-element.7) | copy-start | bytes 196612
  144.0 2.8 %copy-start = (f32[16,8192]{1,0:T(8,128)S(1)}, f32[16,8192]{1,0:T(8,128)}, u32[]{:S(2)}) copy-start(f32[16,8192]{1,0:T(8,128)} %get-tuple-element.14) | copy-start | bytes 1572868

commit v2 on v1

--- a/solution.py
+++ b/solution.py
@@ -61,6 +61,7 @@
     w_buf,
     p_buf,
     r_buf,
+    f_buf,
     xs_buf,
     xr_buf,
     up_buf,
@@ -87,6 +88,7 @@
     w_sem,
     p_send,
     r_sem,
+    f_sem,
     x_send,
     x_sem,
     small_send,
@@ -221,17 +223,104 @@
             to,
         ).start()
 
+    def forward(slot, part, to_slot, to):
+        wait_w(slot, part)
+        send_w(slot, part, to_slot, to)
+
+    def multiply(xh_of, slots):
+        total = None
+        for k in range(2):
+            rows = a_buf[pl.ds(k * 4 + xh_of * 2, 2)].reshape(2 * LEN, KB)
+            cols = [w_buf[slot * 2 + k] for slot in slots]
+            cols = cols[0] if len(cols) == 1 else jnp.concatenate(cols, axis=1)
+            part = dot32(rows, cols, NN_DIMS)
+            total = part if total is None else total + part
+        for i, slot in enumerate(slots):
+            p_buf[pl.ds(slot * 4 + xh_of * 2, 2)] = (
+                total[:, i * 128 : (i + 1) * 128].astype(BF16).reshape(2, LEN, 128)
+            )
+        send_partials(xh_of, slots)
+
+    offset = {0: 0, 1: 7, 2: 1, 3: 6, 4: 2, 5: 5, 6: 3, 7: 4}
+
+    def send_partials(xh_of, slots):
+        side = (xh_of + xh) % 2
+        for slot in slots:
+            owner = (z + offset[slot]) % NZ
+            y_to = owner // 2
+            group = (owner % 2) * 2 + xh_of
+            away = (y_to - y + NY) % NY
+            via = (y + 1 + 2 * side) % NY
+            for c_of in range(2):
+                src = p_buf.at[slot * 4 + xh_of * 2 + c_of]
+
+                @pl.when((away == 0) & (c_of == c))
+                def _():
+                    pltpu.make_async_copy(src, r_buf.at[group, c], r_sem.at[group, c]).start()
+
+                @pl.when((away == 0) & (c_of != c))
+                def _():
+                    remote(src, r_buf.at[group, c], p_send, r_sem.at[group, c], to_core).start()
+
+                @pl.when(away == 2)
+                def _():
+                    index = (side * 2 + owner % 2) * 2 + c_of
+                    remote(
+                        src, f_buf.at[index], p_send, f_sem.at[index], dev(z, via, x, c)
+                    ).start()
+
+                @pl.when(away == 3 - 2 * side)
+                def _():
+                    place = 2 * (1 + away // 3) + c
+                    remote(
+                        src,
+                        r_buf.at[group, place],
+                        p_send,
+                        r_sem.at[group, place],
+                        dev(z, y_to, x, c_of),
+                    ).start()
+
+    def pass_sums(xh_of, slots):
+        side = (xh_of + xh) % 2
+        for slot in slots:
+            owner = (z + offset[slot]) % NZ
+            y_to = owner // 2
+            group = (owner % 2) * 2 + xh_of
+            away = (y_to - y + NY) % NY
+
+            @pl.when(away == 1 + 2 * side)
+            def _():
+                for c_of in range(2):
+                    index = (side * 2 + owner % 2) * 2 + c_of
+                    wait_copy(f_buf.at[index], f_sem.at[index])
+                    f_buf[index] = (
+                        f_buf[index].astype(F32)
+                        + p_buf[slot * 4 + xh_of * 2 + c_of].astype(F32)
+                    ).astype(BF16)
+                    place = 2 * (1 + away // 3) + c
+                    remote(
+                        f_buf.at[index],
+                        r_buf.at[group, place],
+                        p_send,
+                        r_sem.at[group, place],
+                        dev(z, y_to, x, c_of),
+                    ).start()
+
     wait_w(0, 0)
     send_w(0, 0, 1, to_up)
     send_w(0, 0, 2, to_down)
-
+    early_send[0:RANK] = dot32(down_ref[...], a_buf[own], NT_DIMS)
+    wait_w(0, 1)
+    send_w(0, 1, 1, to_up)
+    send_w(0, 1, 2, to_down)
     load_up.wait()
     load_res.wait()
     load_dlt.wait()
-    early_send[0:RANK] = dot32(down_ref[...], a_buf[own], NT_DIMS)
     early_send[RANK : 2 * RANK] = dot32(up_buf[...], res_buf[...], NT_DIMS) + dot32(
         up_buf[...], dlt_buf[...], NT_DIMS
     )
+    forward(1, 0, 3, to_up)
+    forward(2, 0, 4, to_down)
     ones = jnp.ones((8, 128), F32)
     acc_buf[0] = jnp.zeros((LEN, 128), F32)
     for j in range(8):
@@ -244,49 +333,7 @@
             early_send, early_recv.at[t], small_send.at[0], early_sem.at[t], (dp, (t + step) % NT)
         ).start()
     pltpu.make_async_copy(early_send, early_recv.at[t], early_sem.at[t]).start()
-
-    wait_w(0, 1)
-    send_w(0, 1, 1, to_up)
-    send_w(0, 1, 2, to_down)
-
-    def forward(slot, part, to_slot, to):
-        wait_w(slot, part)
-        send_w(slot, part, to_slot, to)
-
-    def multiply(xh_of, slots):
-        total = None
-        for k in range(2):
-            rows = a_buf[pl.ds(k * 4 + xh_of * 2, 2)].reshape(2 * LEN, KB)
-            cols = [w_buf[slot * 2 + k] for slot in slots]
-            cols = cols[0] if len(cols) == 1 else jnp.concatenate(cols, axis=1)
-            part = dot32(rows, cols, NN_DIMS)
-            total = part if total is None else total + part
-        for i, slot in enumerate(slots):
-            p_buf[pl.ds(slot * 4 + xh_of * 2, 2)] = (
-                total[:, i * 128 : (i + 1) * 128].astype(BF16).reshape(2, LEN, 128)
-            )
-        offset = {0: 0, 1: 7, 2: 1, 3: 6, 4: 2, 5: 5, 6: 3, 7: 4}
-        for slot in slots:
-            owner = (z + offset[slot]) % NZ
-            y_to = owner // 2
-            group = (owner % 2) * 2 + xh_of
-            for c_of in range(2):
-                src = p_buf.at[slot * 4 + xh_of * 2 + c_of]
-                dst = r_buf.at[group, y * 2 + c]
-                here = (y_to == y) & (c_of == c)
-
-                @pl.when(here)
-                def _():
-                    pltpu.make_async_copy(src, dst, r_sem.at[group, y * 2 + c]).start()
-
-                @pl.when(jnp.logical_not(here))
-                def _():
-                    remote(
-                        src, dst, p_send, r_sem.at[group, y * 2 + c], dev(z, y_to, x, c_of)
-                    ).start()
-
-    forward(1, 0, 3, to_up)
-    forward(2, 0, 4, to_down)
+    far = (x + 2) % NX
     wait_a_rows(a_index(left, c), 0, 1)
     send_a_rows(a_index(left, c), 0, 5, to_right).start()
     wait_a_rows(a_index(right, c), 1, 4)
@@ -306,35 +353,45 @@
     multiply(xh, (1, 2))
     forward(3, 1, 5, to_up)
     forward(4, 1, 6, to_down)
+    pass_sums(xh, (0,))
     multiply(xh, (3, 4))
-    wait_a_rows(a_index((x + 2) % NX, c), 0, 5)
-    wait_a_rows(a_index((x + 2) % NX, c), 1, 6)
-    send_a_block(a_index((x + 2) % NX, c), 9, to_core).start()
+    pass_sums(xh, (1, 2))
+    wait_a_rows(a_index(far, c), 0, 5)
+    wait_a_rows(a_index(far, c), 1, 6)
+    send_a_block(a_index(far, c), 9, to_core).start()
     forward(5, 0, 7, to_up)
     wait_w(6, 0)
-    wait_a_block(a_index((x + 2) % NX, 1 - c), 9)
+    wait_a_block(a_index(far, 1 - c), 9)
     multiply(1 - xh, (0,))
     multiply(1 - xh, (1, 2))
+    pass_sums(xh, (3, 4))
+    pass_sums(1 - xh, (0,))
     multiply(1 - xh, (3, 4))
+    pass_sums(1 - xh, (1, 2))
     wait_w(5, 1)
     forward(6, 1, 7, to_down)
     multiply(1 - xh, (5, 6))
+    pass_sums(1 - xh, (3, 4))
     multiply(xh, (5, 6))
     wait_w(7, 0)
     wait_w(7, 1)
     multiply(1 - xh, (7,))
     multiply(xh, (7,))
+    pass_sums(1 - xh, (5, 6))
+    pass_sums(xh, (5, 6))
+    pass_sums(1 - xh, (7,))
+    pass_sums(xh, (7,))
 
     for xh_of in range(2):
         for xl_of in range(2):
             group = xl_of * 2 + xh_of
             x_to = xh_of * 2 + xl_of
-            for source in range(8):
+            for source in range(6):
                 wait_copy(r_buf.at[group, source], r_sem.at[group, source])
             for c_of in range(2):
                 total = r_buf[group, c_of].astype(F32)
-                for y_of in range(1, NY):
-                    total = total + r_buf[group, y_of * 2 + c_of].astype(F32)
+                for place in range(1, 3):
+                    total = total + r_buf[group, place * 2 + c_of].astype(F32)
                 xs_buf[x_to, c_of] = total.astype(BF16)
 
             @pl.when(x_to == x)
@@ -453,17 +510,40 @@
 
     pltpu.make_async_copy(h_send, h_recv.at[dp], h_sem.at[dp]).start()
     wait_all(h_recv, h_sem, NDP)
-    gb_rows = h_recv.at[pl.ds(RANK, RANK)]
     for step in range(1, NT):
-        remote(gb_rows, b_recv.at[t], small_send.at[4], b_sem.at[t], (dp, (t + step) % NT)).start()
-    pltpu.make_async_copy(gb_rows, b_recv.at[t], b_sem.at[t]).start()
+        remote(
+            h_recv.at[pl.ds(RANK + 8 * c, 8)],
+            b_recv.at[t, c],
+            small_send.at[4],
+            b_sem.at[t, 0],
+            (dp, (t + step) % NT),
+        ).start()
+    for half in range(2):
+        pltpu.make_async_copy(
+            h_recv.at[pl.ds(RANK + 8 * half, 8)], b_recv.at[t, half], b_sem.at[t, half]
+        ).start()
     for j in range(8):
         ga_ref[:, j * 128 : (j + 1) * 128] = h_recv[0:RANK, j, :]
-    wait_all(b_recv, b_sem, NT)
+    for step in range(1, NT):
+        source = (t + step) % NT
+        wait_copy(b_recv.at[source, c], b_sem.at[source, 0])
+        remote(
+            b_recv.at[source, c],
+            b_recv.at[source, c],
+            small_send.at[4],
+            b_sem.at[source, 1],
+            to_core,
+        ).start()
+    wait_copy(b_recv.at[t, 0], b_sem.at[t, 0])
+    wait_copy(b_recv.at[t, 1], b_sem.at[t, 1])
+    for step in range(1, NT):
+        source = (t + step) % NT
+        wait_copy(b_recv.at[source, 1 - c], b_sem.at[source, 1])
     for t_of in range(NT):
         for j in range(8):
             start = t_of * KB + j * 128
-            gb_ref[:, start : start + 128] = b_recv[t_of, :, j, :]
+            gb_ref[0:8, start : start + 128] = b_recv[t_of, 0, :, j, :]
+            gb_ref[8:16, start : start + 128] = b_recv[t_of, 1, :, j, :]
 
     wait_copy(a_buf.at[pl.ds(0, 7)], a_send)
     wait_copy(w_buf.at[pl.ds(0, 15)], w_send)
@@ -493,7 +573,8 @@
             pltpu.VMEM((8, LEN, KB), BF16),
             pltpu.VMEM((16, KB, 128), BF16),
             pltpu.VMEM((32, LEN, 128), BF16),
-            pltpu.VMEM((4, 8, LEN, 128), BF16),
+            pltpu.VMEM((4, 6, LEN, 128), BF16),
+            pltpu.VMEM((8, LEN, 128), BF16),
             pltpu.VMEM((4, 2, LEN, 128), BF16),
             pltpu.VMEM((4, 2, LEN, 128), BF16),
             pltpu.VMEM((RANK, KB), BF16),
@@ -510,7 +591,7 @@
             pltpu.VMEM((NDP, 8, 128), F32),
             pltpu.VMEM((8, 128), F32),
             pltpu.VMEM((NDP, 8, 128), F32),
-            pltpu.VMEM((NT, RANK, 8, 128), F32),
+            pltpu.VMEM((NT, 2, 8, 8, 128), F32),
             pltpu.VMEM((3, LEN, 128), F32),
             pltpu.SemaphoreType.DMA((4,)),
             pltpu.SemaphoreType.DMA,
@@ -519,7 +600,8 @@
             pltpu.SemaphoreType.DMA,
             pltpu.SemaphoreType.DMA((16,)),
             pltpu.SemaphoreType.DMA,
-            pltpu.SemaphoreType.DMA((4, 8)),
+            pltpu.SemaphoreType.DMA((4, 6)),
+            pltpu.SemaphoreType.DMA((8,)),
             pltpu.SemaphoreType.DMA,
             pltpu.SemaphoreType.DMA((NX,)),
             pltpu.SemaphoreType.DMA((5,)),
@@ -527,7 +609,7 @@
             pltpu.SemaphoreType.DMA((NT,)),
             pltpu.SemaphoreType.DMA((NDP,)),
             pltpu.SemaphoreType.DMA((NDP,)),
-            pltpu.SemaphoreType.DMA((NT,)),
+            pltpu.SemaphoreType.DMA((NT, 2)),
         ],
         compiler_params=pltpu.CompilerParams(
             collective_id=0, has_side_effects=True, vmem_limit_bytes=56 * 1024 * 1024

time: 148 us -> 138 us (0.932)
  Pallas kernels: 143 us -> 133 us
    pallas_call x1, Pallas kernels: 143 us -> 133 us  [local(): pl.pallas_call(kernel, out_shape=(jax.ShapeDtypeStruct((LEN, KB), BF16),...]
where the time goes in v2:
time: 138 us
  Pallas kernels  133 us (96%)
  local copies, waits for them, and re-layouts  3.55 us (3%)
    pallas_call x1, Pallas kernels, local(): pl.pallas_call(kernel, out_shape=(jax.ShapeDtypeStruct((LEN, KB), BF16),...  133 us
    unnamed x7, local copies, waits for them, and re-layouts  3.55 us

profile of v2, /device:TPU:1, one launch (start us, length us, event | category | flops | bytes accessed | tf_op | source)
XLA Modules:
  0.0 137.7 jit_solution(18388163187190417451)
XLA Ops:
  0.6 133.5 %shard_map.103 = (bf16[384,1024]{1,0:T(8,128)(2,1)}, f32[16,1024]{1,0:T(8,128)}, f32[16,8192]{1,0:T(8,128)}) custom-call(bf16[384,1024]{1,0:T(8,128)(2,1)} %ctx_hbm.1, bf16[1024,256]{1,0:T(8,128)(2,1)} %w_hbm.1, bf16[16,1024]{1,0:T(8,128)(2,1)} %bitcast.5, bf16[16,8192]{1,0:T(8,128)(2,1)} %up_hbm.1, bf16[384,1024]{1,0:T(8,128)(2,1)} %res_hbm.1, ...), custom_call_target="tpu_custom_call" | custom-call | tf_op jit(solution)/shard_map/pallas_call | solution.py:563
  134.1 0.0 copy-start.1
  134.1 0.0 copy-start
  134.1 2.1 %copy.14 = bf16[384,1024]{1,0:T(8,128)(2,1)} copy(bf16[384,1024]{1,0:T(8,128)(2,1)} %get-tuple-element.12) | data formatting | bytes 1572864
  136.3 0.0 copy-done.1
  136.3 0.6 copy.15
  136.9 0.0 copy-done
  136.9 0.8 copy.16
Async XLA Ops:
  134.1 2.1 %copy-start.1 = (f32[16,1024]{1,0:T(8,128)S(1)}, f32[16,1024]{1,0:T(8,128)}, u32[]{:S(2)}) copy-start(f32[16,1024]{1,0:T(8,128)} %get-tuple-element.7) | copy-start | bytes 196612
  134.1 2.8 %copy-start = (f32[16,8192]{1,0:T(8,128)S(1)}, f32[16,8192]{1,0:T(8,128)}, u32[]{:S(2)}) copy-start(f32[16,8192]{1,0:T(8,128)} %get-tuple-element.14) | copy-start | bytes 1572868

commit v3 on v2

--- a/solution.py
+++ b/solution.py
@@ -163,15 +163,18 @@
 
     for step in range(1, NY):
         greet(dev(z, (y + step) % NY, x, 1 - c))
-    greet(dev(z, y, 2 * (1 - xh) + (1 - xl), c))
     for step in range(1, NT):
         greet((dp, (t + step) % NT))
-
-    @pl.loop(1, NDP)
-    def _(step):
-        greet(((dp + step) % NDP, t))
-
-    pl.semaphore_wait(barrier, (NY - 1) + 1 + (NT - 1) + (NDP - 1))
+    for near in (
+        to_core,
+        to_up,
+        to_down,
+        dev(z, y, 2 * (1 - xh) + (1 - xl), c),
+        dev(z, y, 2 * (1 - xh) + xl, c),
+        dev(z, y, 2 * (1 - xh) + xl, 1 - c),
+    ):
+        greet(near)
+    pl.semaphore_wait(barrier, (NY - 1) + (NT - 1) + 6)
 
     send_pair = remote(
         w_hbm.at[:, pl.ds(pl.multiple_of((1 - xl) * 128, 128), 128)],
@@ -353,9 +356,7 @@
     multiply(xh, (1, 2))
     forward(3, 1, 5, to_up)
     forward(4, 1, 6, to_down)
-    pass_sums(xh, (0,))
     multiply(xh, (3, 4))
-    pass_sums(xh, (1, 2))
     wait_a_rows(a_index(far, c), 0, 5)
     wait_a_rows(a_index(far, c), 1, 6)
     send_a_block(a_index(far, c), 9, to_core).start()
@@ -363,24 +364,26 @@
     wait_w(6, 0)
     wait_a_block(a_index(far, 1 - c), 9)
     multiply(1 - xh, (0,))
+    pass_sums(xh, (0,))
     multiply(1 - xh, (1, 2))
-    pass_sums(xh, (3, 4))
-    pass_sums(1 - xh, (0,))
-    multiply(1 - xh, (3, 4))
-    pass_sums(1 - xh, (1, 2))
+    pass_sums(xh, (1, 2))
     wait_w(5, 1)
     forward(6, 1, 7, to_down)
+    multiply(1 - xh, (3, 4))
+    pass_sums(xh, (3, 4))
+    multiply(xh, (5, 6))
+    pass_sums(1 - xh, (0,))
     multiply(1 - xh, (5, 6))
-    pass_sums(1 - xh, (3, 4))
-    multiply(xh, (5, 6))
+    pass_sums(1 - xh, (1, 2))
     wait_w(7, 0)
     wait_w(7, 1)
+    multiply(xh, (7,))
     multiply(1 - xh, (7,))
-    multiply(xh, (7,))
+    pass_sums(1 - xh, (3, 4))
+    pass_sums(xh, (5, 6))
     pass_sums(1 - xh, (5, 6))
-    pass_sums(xh, (5, 6))
+    pass_sums(xh, (7,))
     pass_sums(1 - xh, (7,))
-    pass_sums(xh, (7,))
 
     for xh_of in range(2):
         for xl_of in range(2):
@@ -413,26 +416,26 @@
     sq_target = early[2 * RANK : 2 * RANK + 1]
     low3 = split3(2.0 * low_rank)
 
-    for source in range(NX):
-        wait_copy(xr_buf.at[source], x_sem.at[source])
     for i in range(3):
         acc_buf[i] = jnp.zeros((LEN, 128), F32)
-    for j in range(8):
-        cols = pl.ds(j * 128, 128)
-        x_of = (j // 4) * 2 + j % 2
-        c_of = (j // 2) % 2
-        up3 = jnp.concatenate([up_buf[:, cols]] * 3, axis=0)
-        res = res_buf[:, cols].astype(F32)
-        state = res + xr_buf[x_of, c_of].astype(F32) + dot32(low3, up3, TN_DIMS)
-        ad_buf[:, cols] = state.astype(BF16)
-        target = res + dlt_buf[:, cols].astype(F32)
-        gap = state - target
-        acc_buf[0] += state * state
-        acc_buf[1] += state * target
-        acc_buf[2] += gap * gap
-        high = gap.astype(BF16)
-        ghi_buf[:, cols] = high
-        glo_buf[:, cols] = (gap - high.astype(F32)).astype(BF16)
+    for turn in (0, 1, 3, 2):
+        x_of = (x + turn) % NX
+        wait_copy(xr_buf.at[x_of], x_sem.at[x_of])
+        for c_of in range(2):
+            start = ((x_of // 2) * 4 + c_of * 2 + x_of % 2) * 128
+            cols = pl.ds(pl.multiple_of(start, 128), 128)
+            up3 = jnp.concatenate([up_buf[:, cols]] * 3, axis=0)
+            res = res_buf[:, cols].astype(F32)
+            state = res + xr_buf[x_of, c_of].astype(F32) + dot32(low3, up3, TN_DIMS)
+            ad_buf[:, cols] = state.astype(BF16)
+            target = res + dlt_buf[:, cols].astype(F32)
+            gap = state - target
+            acc_buf[0] += state * state
+            acc_buf[1] += state * target
+            acc_buf[2] += gap * gap
+            high = gap.astype(BF16)
+            ghi_buf[:, cols] = high
+            glo_buf[:, cols] = (gap - high.astype(F32)).astype(BF16)
     store_adapted = pltpu.make_async_copy(ad_buf, adapted_hbm, out_sem)
     store_adapted.start()
     late_send[0:RANK] = dot32(up_buf[...], ghi_buf[...], NT_DIMS) + dot32(

time: 138 us -> 133 us (0.964)
  Pallas kernels: 133 us -> 128 us
    pallas_call x1, Pallas kernels: 133 us -> 128 us  [local(): pl.pallas_call(kernel, out_shape=(jax.ShapeDtypeStruct((LEN, KB), BF16),...]
where the time goes in v3:
time: 133 us
  Pallas kernels  128 us (96%)
  local copies, waits for them, and re-layouts  3.55 us (3%)
    pallas_call x1, Pallas kernels, local(): pl.pallas_call(kernel, out_shape=(jax.ShapeDtypeStruct((LEN, KB), BF16),...  128 us
    unnamed x7, local copies, waits for them, and re-layouts  3.55 us

profile of v3, /device:TPU:1, one launch (start us, length us, event | category | flops | bytes accessed | tf_op | source)
XLA Modules:
  0.0 132.5 jit_solution(18155564169247059382)
XLA Ops:
  0.6 128.3 %shard_map.103 = (bf16[384,1024]{1,0:T(8,128)(2,1)}, f32[16,1024]{1,0:T(8,128)}, f32[16,8192]{1,0:T(8,128)}) custom-call(bf16[384,1024]{1,0:T(8,128)(2,1)} %ctx_hbm.1, bf16[1024,256]{1,0:T(8,128)(2,1)} %w_hbm.1, bf16[16,1024]{1,0:T(8,128)(2,1)} %bitcast.5, bf16[16,8192]{1,0:T(8,128)(2,1)} %up_hbm.1, bf16[384,1024]{1,0:T(8,128)(2,1)} %res_hbm.1, ...), custom_call_target="tpu_custom_call" | custom-call | tf_op jit(solution)/shard_map/pallas_call | solution.py:566
  129.0 0.0 copy-start.1
  129.0 0.0 copy-start
  129.0 2.1 %copy.14 = bf16[384,1024]{1,0:T(8,128)(2,1)} copy(bf16[384,1024]{1,0:T(8,128)(2,1)} %get-tuple-element.12) | data formatting | bytes 1572864
  131.1 0.0 copy-done.1
  131.1 0.6 copy.15
  131.8 0.0 copy-done
  131.8 0.8 copy.16
Async XLA Ops:
  129.0 2.1 %copy-start.1 = (f32[16,1024]{1,0:T(8,128)S(1)}, f32[16,1024]{1,0:T(8,128)}, u32[]{:S(2)}) copy-start(f32[16,1024]{1,0:T(8,128)} %get-tuple-element.7) | copy-start | bytes 196612
  129.0 2.8 %copy-start = (f32[16,8192]{1,0:T(8,128)S(1)}, f32[16,8192]{1,0:T(8,128)}, u32[]{:S(2)}) copy-start(f32[16,8192]{1,0:T(8,128)} %get-tuple-element.14) | copy-start | bytes 1572868

commit v4 on v3

--- a/solution.py
+++ b/solution.py
@@ -246,16 +246,24 @@
 
     offset = {0: 0, 1: 7, 2: 1, 3: 6, 4: 2, 5: 5, 6: 3, 7: 4}
 
+    def route(xh_of, slot):
+        side = (xh_of + xh) % 2
+        owner = (z + offset[slot]) % NZ
+        group = (owner % 2) * 2 + xh_of
+        away = ((owner // 2 - y + NY) * (1 + 2 * side)) % NY
+        onward = (y + 1 + 2 * side) % NY
+
+        def place(stage, c_of):
+            return ((side * 2 + stage) * 2 + owner % 2) * 2 + c_of
+
+        return group, away, onward, place
+
     def send_partials(xh_of, slots):
-        side = (xh_of + xh) % 2
         for slot in slots:
-            owner = (z + offset[slot]) % NZ
-            y_to = owner // 2
-            group = (owner % 2) * 2 + xh_of
-            away = (y_to - y + NY) % NY
-            via = (y + 1 + 2 * side) % NY
+            group, away, onward, place = route(xh_of, slot)
             for c_of in range(2):
                 src = p_buf.at[slot * 4 + xh_of * 2 + c_of]
+                start = place(0, c_of)
 
                 @pl.when((away == 0) & (c_of == c))
                 def _():
@@ -265,48 +273,43 @@
                 def _():
                     remote(src, r_buf.at[group, c], p_send, r_sem.at[group, c], to_core).start()
 
-                @pl.when(away == 2)
+                @pl.when(away == 3)
                 def _():
-                    index = (side * 2 + owner % 2) * 2 + c_of
                     remote(
-                        src, f_buf.at[index], p_send, f_sem.at[index], dev(z, via, x, c)
+                        src, f_buf.at[start], p_send, f_sem.at[start], dev(z, onward, x, c)
                     ).start()
 
-                @pl.when(away == 3 - 2 * side)
-                def _():
-                    place = 2 * (1 + away // 3) + c
-                    remote(
-                        src,
-                        r_buf.at[group, place],
-                        p_send,
-                        r_sem.at[group, place],
-                        dev(z, y_to, x, c_of),
-                    ).start()
-
     def pass_sums(xh_of, slots):
-        side = (xh_of + xh) % 2
         for slot in slots:
-            owner = (z + offset[slot]) % NZ
-            y_to = owner // 2
-            group = (owner % 2) * 2 + xh_of
-            away = (y_to - y + NY) % NY
-
-            @pl.when(away == 1 + 2 * side)
+            group, away, onward, place = route(xh_of, slot)
+
+            def add(index, c_of):
+                wait_copy(f_buf.at[index], f_sem.at[index])
+                f_buf[index] = (
+                    f_buf[index].astype(F32) + p_buf[slot * 4 + xh_of * 2 + c_of].astype(F32)
+                ).astype(BF16)
+
+            @pl.when(away == 2)
             def _():
                 for c_of in range(2):
-                    index = (side * 2 + owner % 2) * 2 + c_of
-                    wait_copy(f_buf.at[index], f_sem.at[index])
-                    f_buf[index] = (
-                        f_buf[index].astype(F32)
-                        + p_buf[slot * 4 + xh_of * 2 + c_of].astype(F32)
-                    ).astype(BF16)
-                    place = 2 * (1 + away // 3) + c
+                    index = place(0, c_of)
+                    after = place(1, c_of)
+                    add(index, c_of)
+                    remote(
+                        f_buf.at[index], f_buf.at[after], p_send, f_sem.at[after], dev(z, onward, x, c)
+                    ).start()
+
+            @pl.when(away == 1)
+            def _():
+                for c_of in range(2):
+                    index = place(1, c_of)
+                    add(index, c_of)
                     remote(
                         f_buf.at[index],
-                        r_buf.at[group, place],
+                        r_buf.at[group, 2 + c],
                         p_send,
-                        r_sem.at[group, place],
-                        dev(z, y_to, x, c_of),
+                        r_sem.at[group, 2 + c],
+                        dev(z, onward, x, c_of),
                     ).start()
 
     wait_w(0, 0)
@@ -377,35 +380,28 @@
     pass_sums(1 - xh, (1, 2))
     wait_w(7, 0)
     wait_w(7, 1)
+    multiply(1 - xh, (7,))
     multiply(xh, (7,))
-    multiply(1 - xh, (7,))
     pass_sums(1 - xh, (3, 4))
+    pass_sums(1 - xh, (5, 6))
     pass_sums(xh, (5, 6))
-    pass_sums(1 - xh, (5, 6))
+    pass_sums(1 - xh, (7,))
     pass_sums(xh, (7,))
-    pass_sums(1 - xh, (7,))
-
-    for xh_of in range(2):
-        for xl_of in range(2):
-            group = xl_of * 2 + xh_of
-            x_to = xh_of * 2 + xl_of
-            for source in range(6):
-                wait_copy(r_buf.at[group, source], r_sem.at[group, source])
-            for c_of in range(2):
-                total = r_buf[group, c_of].astype(F32)
-                for place in range(1, 3):
-                    total = total + r_buf[group, place * 2 + c_of].astype(F32)
-                xs_buf[x_to, c_of] = total.astype(BF16)
-
-            @pl.when(x_to == x)
-            def _():
-                pltpu.make_async_copy(xs_buf.at[x_to], xr_buf.at[x], x_sem.at[x]).start()
-
-            @pl.when(x_to != x)
-            def _():
-                remote(
-                    xs_buf.at[x_to], xr_buf.at[x], x_send, x_sem.at[x], dev(z, y, x_to, c)
-                ).start()
+
+    for turn in (2, 1, 3, 0):
+        x_to = (x + turn) % NX
+        group = (x_to % 2) * 2 + x_to // 2
+        for source in range(4):
+            wait_copy(r_buf.at[group, source], r_sem.at[group, source])
+        for c_of in range(2):
+            total = r_buf[group, c_of].astype(F32) + r_buf[group, 2 + c_of].astype(F32)
+            xs_buf[x_to, c_of] = total.astype(BF16)
+        if turn == 0:
+            pltpu.make_async_copy(xs_buf.at[x_to], xr_buf.at[x], x_sem.at[x]).start()
+        else:
+            remote(
+                xs_buf.at[x_to], xr_buf.at[x], x_send, x_sem.at[x], dev(z, y, x_to, c)
+            ).start()
 
     wait_all(early_recv, early_sem, NT)
     early = early_recv[0]
@@ -441,8 +437,12 @@
     late_send[0:RANK] = dot32(up_buf[...], ghi_buf[...], NT_DIMS) + dot32(
         up_buf[...], glo_buf[...], NT_DIMS
     )
+    row = lax.broadcasted_iota(jnp.int32, (8, 128), 0)
+    stats = None
     for i in range(3):
-        late_send[RANK + 8 * i : RANK + 8 * i + 8] = dot_high(ones, acc_buf[i], NT_DIMS)
+        part = dot_high((row == i).astype(F32), acc_buf[i], NT_DIMS)
+        stats = part if stats is None else stats + part
+    late_send[RANK:] = stats
     for step in range(1, NT):
         remote(
             late_send, late_recv.at[t], small_send.at[1], late_sem.at[t], (dp, (t + step) % NT)
@@ -470,8 +470,8 @@
         late = late + late_recv[other]
     gap_up = late[0:RANK]
     norm_h = jnp.sqrt(late[RANK : RANK + 1] + NORM_EPS)
-    cross = late[RANK + 8 : RANK + 9]
-    distance = jnp.sqrt(late[RANK + 16 : RANK + 17] + NORM_EPS)
+    cross = late[RANK + 1 : RANK + 2]
+    distance = jnp.sqrt(late[RANK + 2 : RANK + 3] + NORM_EPS)
     norm_g = jnp.sqrt(sq_target + NORM_EPS)
     cosine = cross / (norm_h * norm_g)
     first = weight_harm / (norm_h * norm_g)
@@ -576,8 +576,8 @@
             pltpu.VMEM((8, LEN, KB), BF16),
             pltpu.VMEM((16, KB, 128), BF16),
             pltpu.VMEM((32, LEN, 128), BF16),
-            pltpu.VMEM((4, 6, LEN, 128), BF16),
-            pltpu.VMEM((8, LEN, 128), BF16),
+            pltpu.VMEM((4, 4, LEN, 128), BF16),
+            pltpu.VMEM((16, LEN, 128), BF16),
             pltpu.VMEM((4, 2, LEN, 128), BF16),
             pltpu.VMEM((4, 2, LEN, 128), BF16),
             pltpu.VMEM((RANK, KB), BF16),
@@ -588,8 +588,8 @@
             pltpu.VMEM((LEN, KB), BF16),
             pltpu.VMEM((40, LEN), F32),
             pltpu.VMEM((NT, 40, LEN), F32),
-            pltpu.VMEM((40, LEN), F32),
-            pltpu.VMEM((NT, 40, LEN), F32),
+            pltpu.VMEM((24, LEN), F32),
+            pltpu.VMEM((NT, 24, LEN), F32),
             pltpu.VMEM((NDP, 8, 128), F32),
             pltpu.VMEM((NDP, 8, 128), F32),
             pltpu.VMEM((8, 128), F32),
@@ -603,8 +603,8 @@
             pltpu.SemaphoreType.DMA,
             pltpu.SemaphoreType.DMA((16,)),
             pltpu.SemaphoreType.DMA,
-            pltpu.SemaphoreType.DMA((4, 6)),
-            pltpu.SemaphoreType.DMA((8,)),
+            pltpu.SemaphoreType.DMA((4, 4)),
+            pltpu.SemaphoreType.DMA((16,)),
             pltpu.SemaphoreType.DMA,
             pltpu.SemaphoreType.DMA((NX,)),
             pltpu.SemaphoreType.DMA((5,)),

time: 133 us -> 169 us (1.27)
  Pallas kernels: 128 us -> 164 us
    pallas_call x1, Pallas kernels: 128 us -> 164 us  [local(): pl.pallas_call(kernel, out_shape=(jax.ShapeDtypeStruct((LEN, KB), BF16),...]
where the time goes in v4:
time: 169 us
  Pallas kernels  164 us (97%)
  local copies, waits for them, and re-layouts  3.55 us (2%)
    pallas_call x1, Pallas kernels, local(): pl.pallas_call(kernel, out_shape=(jax.ShapeDtypeStruct((LEN, KB), BF16),...  164 us
    unnamed x7, local copies, waits for them, and re-layouts  3.55 us

profile of v4, /device:TPU:1, one launch (start us, length us, event | category | flops | bytes accessed | tf_op | source)
XLA Modules:
  0.0 168.5 jit_solution(17361779324331332283)
XLA Ops:
  0.6 164.3 %shard_map.103 = (bf16[384,1024]{1,0:T(8,128)(2,1)}, f32[16,1024]{1,0:T(8,128)}, f32[16,8192]{1,0:T(8,128)}) custom-call(bf16[384,1024]{1,0:T(8,128)(2,1)} %ctx_hbm.1, bf16[1024,256]{1,0:T(8,128)(2,1)} %w_hbm.1, bf16[16,1024]{1,0:T(8,128)(2,1)} %bitcast.5, bf16[16,8192]{1,0:T(8,128)(2,1)} %up_hbm.1, bf16[384,1024]{1,0:T(8,128)(2,1)} %res_hbm.1, ...), custom_call_target="tpu_custom_call" | custom-call | tf_op jit(solution)/shard_map/pallas_call | solution.py:566
  164.9 0.0 copy-start.1
  164.9 0.0 copy-start
  164.9 2.1 %copy.14 = bf16[384,1024]{1,0:T(8,128)(2,1)} copy(bf16[384,1024]{1,0:T(8,128)(2,1)} %get-tuple-element.12) | data formatting | bytes 1572864
  167.1 0.0 copy-done.1
  167.1 0.6 copy.15
  167.7 0.0 copy-done
  167.7 0.8 copy.16
Async XLA Ops:
  164.9 2.1 %copy-start.1 = (f32[16,1024]{1,0:T(8,128)S(1)}, f32[16,1024]{1,0:T(8,128)}, u32[]{:S(2)}) copy-start(f32[16,1024]{1,0:T(8,128)} %get-tuple-element.7) | copy-start | bytes 196612
  164.9 2.8 %copy-start = (f32[16,8192]{1,0:T(8,128)S(1)}, f32[16,8192]{1,0:T(8,128)}, u32[]{:S(2)}) copy-start(f32[16,8192]{1,0:T(8,128)} %get-tuple-element.14) | copy-start | bytes 1572868

commit v5 on v3

--- a/solution.py
+++ b/solution.py
@@ -364,48 +364,43 @@
     wait_w(6, 0)
     wait_a_block(a_index(far, 1 - c), 9)
     multiply(1 - xh, (0,))
-    pass_sums(xh, (0,))
     multiply(1 - xh, (1, 2))
-    pass_sums(xh, (1, 2))
+    multiply(1 - xh, (3, 4))
     wait_w(5, 1)
     forward(6, 1, 7, to_down)
-    multiply(1 - xh, (3, 4))
+    multiply(1 - xh, (5, 6))
+    multiply(xh, (5, 6))
+    pass_sums(xh, (0,))
+    pass_sums(xh, (1, 2))
     pass_sums(xh, (3, 4))
-    multiply(xh, (5, 6))
-    pass_sums(1 - xh, (0,))
-    multiply(1 - xh, (5, 6))
-    pass_sums(1 - xh, (1, 2))
     wait_w(7, 0)
     wait_w(7, 1)
+    multiply(1 - xh, (7,))
     multiply(xh, (7,))
-    multiply(1 - xh, (7,))
+    pass_sums(1 - xh, (0,))
+    pass_sums(1 - xh, (1, 2))
     pass_sums(1 - xh, (3, 4))
+    pass_sums(1 - xh, (5, 6))
     pass_sums(xh, (5, 6))
-    pass_sums(1 - xh, (5, 6))
+    pass_sums(1 - xh, (7,))
     pass_sums(xh, (7,))
-    pass_sums(1 - xh, (7,))
-
-    for xh_of in range(2):
-        for xl_of in range(2):
-            group = xl_of * 2 + xh_of
-            x_to = xh_of * 2 + xl_of
-            for source in range(6):
-                wait_copy(r_buf.at[group, source], r_sem.at[group, source])
-            for c_of in range(2):
-                total = r_buf[group, c_of].astype(F32)
-                for place in range(1, 3):
-                    total = total + r_buf[group, place * 2 + c_of].astype(F32)
-                xs_buf[x_to, c_of] = total.astype(BF16)
-
-            @pl.when(x_to == x)
-            def _():
-                pltpu.make_async_copy(xs_buf.at[x_to], xr_buf.at[x], x_sem.at[x]).start()
-
-            @pl.when(x_to != x)
-            def _():
-                remote(
-                    xs_buf.at[x_to], xr_buf.at[x], x_send, x_sem.at[x], dev(z, y, x_to, c)
-                ).start()
+
+    for turn in (2, 1, 3, 0):
+        x_to = (x + turn) % NX
+        group = (x_to % 2) * 2 + x_to // 2
+        for source in range(6):
+            wait_copy(r_buf.at[group, source], r_sem.at[group, source])
+        for c_of in range(2):
+            total = r_buf[group, c_of].astype(F32)
+            for place in range(1, 3):
+                total = total + r_buf[group, place * 2 + c_of].astype(F32)
+            xs_buf[x_to, c_of] = total.astype(BF16)
+        if turn == 0:
+            pltpu.make_async_copy(xs_buf.at[x_to], xr_buf.at[x], x_sem.at[x]).start()
+        else:
+            remote(
+                xs_buf.at[x_to], xr_buf.at[x], x_send, x_sem.at[x], dev(z, y, x_to, c)
+            ).start()
 
     wait_all(early_recv, early_sem, NT)
     early = early_recv[0]
@@ -441,8 +436,12 @@
     late_send[0:RANK] = dot32(up_buf[...], ghi_buf[...], NT_DIMS) + dot32(
         up_buf[...], glo_buf[...], NT_DIMS
     )
+    row = lax.broadcasted_iota(jnp.int32, (8, 128), 0)
+    stats = None
     for i in range(3):
-        late_send[RANK + 8 * i : RANK + 8 * i + 8] = dot_high(ones, acc_buf[i], NT_DIMS)
+        part = dot_high((row == i).astype(F32), acc_buf[i], NT_DIMS)
+        stats = part if stats is None else stats + part
+    late_send[RANK:] = stats
     for step in range(1, NT):
         remote(
             late_send, late_recv.at[t], small_send.at[1], late_sem.at[t], (dp, (t + step) % NT)
@@ -470,8 +469,8 @@
         late = late + late_recv[other]
     gap_up = late[0:RANK]
     norm_h = jnp.sqrt(late[RANK : RANK + 1] + NORM_EPS)
-    cross = late[RANK + 8 : RANK + 9]
-    distance = jnp.sqrt(late[RANK + 16 : RANK + 17] + NORM_EPS)
+    cross = late[RANK + 1 : RANK + 2]
+    distance = jnp.sqrt(late[RANK + 2 : RANK + 3] + NORM_EPS)
     norm_g = jnp.sqrt(sq_target + NORM_EPS)
     cosine = cross / (norm_h * norm_g)
     first = weight_harm / (norm_h * norm_g)
@@ -588,8 +587,8 @@
             pltpu.VMEM((LEN, KB), BF16),
             pltpu.VMEM((40, LEN), F32),
             pltpu.VMEM((NT, 40, LEN), F32),
-            pltpu.VMEM((40, LEN), F32),
-            pltpu.VMEM((NT, 40, LEN), F32),
+            pltpu.VMEM((24, LEN), F32),
+            pltpu.VMEM((NT, 24, LEN), F32),
             pltpu.VMEM((NDP, 8, 128), F32),
             pltpu.VMEM((NDP, 8, 128), F32),
             pltpu.VMEM((8, 128), F32),

time: 133 us -> 130 us (0.977)
  Pallas kernels: 128 us -> 126 us
    pallas_call x1, Pallas kernels: 128 us -> 126 us  [local(): pl.pallas_call(kernel, out_shape=(jax.ShapeDtypeStruct((LEN, KB), BF16),...]
where the time goes in v5:
time: 130 us
  Pallas kernels  126 us (97%)
  local copies, waits for them, and re-layouts  3.55 us (3%)
    pallas_call x1, Pallas kernels, local(): pl.pallas_call(kernel, out_shape=(jax.ShapeDtypeStruct((LEN, KB), BF16),...  126 us
    unnamed x7, local copies, waits for them, and re-layouts  3.55 us

profile of v5, /device:TPU:1, one launch (start us, length us, event | category | flops | bytes accessed | tf_op | source)
XLA Modules:
  0.0 129.8 jit_solution(2676500737954154905)
XLA Ops:
  0.6 125.6 %shard_map.103 = (bf16[384,1024]{1,0:T(8,128)(2,1)}, f32[16,1024]{1,0:T(8,128)}, f32[16,8192]{1,0:T(8,128)}) custom-call(bf16[384,1024]{1,0:T(8,128)(2,1)} %ctx_hbm.1, bf16[1024,256]{1,0:T(8,128)(2,1)} %w_hbm.1, bf16[16,1024]{1,0:T(8,128)(2,1)} %bitcast.5, bf16[16,8192]{1,0:T(8,128)(2,1)} %up_hbm.1, bf16[384,1024]{1,0:T(8,128)(2,1)} %res_hbm.1, ...), custom_call_target="tpu_custom_call" | custom-call | tf_op jit(solution)/shard_map/pallas_call | solution.py:565
  126.3 0.0 copy-start.1
  126.3 0.0 copy-start
  126.3 2.1 %copy.14 = bf16[384,1024]{1,0:T(8,128)(2,1)} copy(bf16[384,1024]{1,0:T(8,128)(2,1)} %get-tuple-element.12) | data formatting | bytes 1572864
  128.4 0.0 copy-done.1
  128.4 0.6 copy.15
  129.0 0.0 copy-done
  129.0 0.8 copy.16
Async XLA Ops:
  126.3 2.1 %copy-start.1 = (f32[16,1024]{1,0:T(8,128)S(1)}, f32[16,1024]{1,0:T(8,128)}, u32[]{:S(2)}) copy-start(f32[16,1024]{1,0:T(8,128)} %get-tuple-element.7) | copy-start | bytes 196612
  126.3 2.8 %copy-start = (f32[16,8192]{1,0:T(8,128)S(1)}, f32[16,8192]{1,0:T(8,128)}, u32[]{:S(2)}) copy-start(f32[16,8192]{1,0:T(8,128)} %get-tuple-element.14) | copy-start | bytes 1572868

commit v6 on v5

--- a/solution.py
+++ b/solution.py
@@ -324,13 +324,13 @@
     )
     forward(1, 0, 3, to_up)
     forward(2, 0, 4, to_down)
-    ones = jnp.ones((8, 128), F32)
+    row = lax.broadcasted_iota(jnp.int32, (8, 128), 0)
     acc_buf[0] = jnp.zeros((LEN, 128), F32)
     for j in range(8):
         cols = pl.ds(j * 128, 128)
         target = res_buf[:, cols].astype(F32) + dlt_buf[:, cols].astype(F32)
         acc_buf[0] += target * target
-    early_send[2 * RANK :] = dot_high(ones, acc_buf[0], NT_DIMS)
+    target_stats = dot_high((row == 3).astype(F32), acc_buf[0], NT_DIMS)
     for step in range(1, NT):
         remote(
             early_send, early_recv.at[t], small_send.at[0], early_sem.at[t], (dp, (t + step) % NT)
@@ -408,7 +408,6 @@
         early = early + early_recv[other]
     low_rank = early[0:RANK]
     target_up = early[RANK : 2 * RANK]
-    sq_target = early[2 * RANK : 2 * RANK + 1]
     low3 = split3(2.0 * low_rank)
 
     for i in range(3):
@@ -436,11 +435,9 @@
     late_send[0:RANK] = dot32(up_buf[...], ghi_buf[...], NT_DIMS) + dot32(
         up_buf[...], glo_buf[...], NT_DIMS
     )
-    row = lax.broadcasted_iota(jnp.int32, (8, 128), 0)
-    stats = None
+    stats = target_stats
     for i in range(3):
-        part = dot_high((row == i).astype(F32), acc_buf[i], NT_DIMS)
-        stats = part if stats is None else stats + part
+        stats = stats + dot_high((row == i).astype(F32), acc_buf[i], NT_DIMS)
     late_send[RANK:] = stats
     for step in range(1, NT):
         remote(
@@ -471,7 +468,7 @@
     norm_h = jnp.sqrt(late[RANK : RANK + 1] + NORM_EPS)
     cross = late[RANK + 1 : RANK + 2]
     distance = jnp.sqrt(late[RANK + 2 : RANK + 3] + NORM_EPS)
-    norm_g = jnp.sqrt(sq_target + NORM_EPS)
+    norm_g = jnp.sqrt(late[RANK + 3 : RANK + 4] + NORM_EPS)
     cosine = cross / (norm_h * norm_g)
     first = weight_harm / (norm_h * norm_g)
     second = weight_harm * cosine / (norm_h * norm_h)
@@ -585,8 +582,8 @@
             pltpu.VMEM((LEN, KB), BF16),
             pltpu.VMEM((LEN, KB), BF16),
             pltpu.VMEM((LEN, KB), BF16),
-            pltpu.VMEM((40, LEN), F32),
-            pltpu.VMEM((NT, 40, LEN), F32),
+            pltpu.VMEM((32, LEN), F32),
+            pltpu.VMEM((NT, 32, LEN), F32),
             pltpu.VMEM((24, LEN), F32),
             pltpu.VMEM((NT, 24, LEN), F32),
             pltpu.VMEM((NDP, 8, 128), F32),

time: 130 us -> 129 us (level)
  no operation moved by 1% of the time
where the time goes in v6:
time: 129 us
  Pallas kernels  125 us (97%)
  local copies, waits for them, and re-layouts  3.55 us (3%)
    pallas_call x1, Pallas kernels, local(): pl.pallas_call(kernel, out_shape=(jax.ShapeDtypeStruct((LEN, KB), BF16),...  125 us
    unnamed x7, local copies, waits for them, and re-layouts  3.55 us

profile of v6, /device:TPU:1, one launch (start us, length us, event | category | flops | bytes accessed | tf_op | source)
XLA Modules:
  0.0 128.8 jit_solution(7077481016191798787)
XLA Ops:
  0.6 124.6 %shard_map.103 = (bf16[384,1024]{1,0:T(8,128)(2,1)}, f32[16,1024]{1,0:T(8,128)}, f32[16,8192]{1,0:T(8,128)}) custom-call(bf16[384,1024]{1,0:T(8,128)(2,1)} %ctx_hbm.1, bf16[1024,256]{1,0:T(8,128)(2,1)} %w_hbm.1, bf16[16,1024]{1,0:T(8,128)(2,1)} %bitcast.5, bf16[16,8192]{1,0:T(8,128)(2,1)} %up_hbm.1, bf16[384,1024]{1,0:T(8,128)(2,1)} %res_hbm.1, ...), custom_call_target="tpu_custom_call" | custom-call | tf_op jit(solution)/shard_map/pallas_call | solution.py:562
  125.2 0.0 copy-start.1
  125.3 0.0 copy-start
  125.3 2.1 %copy.14 = bf16[384,1024]{1,0:T(8,128)(2,1)} copy(bf16[384,1024]{1,0:T(8,128)(2,1)} %get-tuple-element.12) | data formatting | bytes 1572864
  127.4 0.0 copy-done.1
  127.4 0.6 copy.15
  128.0 0.0 copy-done
  128.0 0.8 copy.16
Async XLA Ops:
  125.2 2.1 %copy-start.1 = (f32[16,1024]{1,0:T(8,128)S(1)}, f32[16,1024]{1,0:T(8,128)}, u32[]{:S(2)}) copy-start(f32[16,1024]{1,0:T(8,128)} %get-tuple-element.7) | copy-start | bytes 196612
  125.3 2.8 %copy-start = (f32[16,8192]{1,0:T(8,128)S(1)}, f32[16,8192]{1,0:T(8,128)}, u32[]{:S(2)}) copy-start(f32[16,8192]{1,0:T(8,128)} %get-tuple-element.14) | copy-start | bytes 1572868
